TPU v7x, 256 devices: a whole 4x4x8 slice. The times are simulated.
256 devices in a mesh: row: 16 (over z, core), col: 16 (over x, y).
Axes of the slice: x: 4, y: 4, z: 8, core: 2. Of those that a mesh axis runs over, the one named last changes fastest.
Arguments:
- inputs: bfloat16 [4096, 18432], P('col', 'row'), may hold values from -6 to 6
- out_grads: bfloat16 [4096, 18432], P('row', 'col'), may hold values from -0.09375 to 0.09375
- range_test: float32 [18432, 128], P('col'), may hold values from -0.046875 to 0.046875
- corange_test: float32 [256, 18432], P(None, 'row'), may hold values from -0.046875 to 0.046875
Outputs:
- range_sketch: float32 [18432, 128], P('row')
- corange_sketch: float32 [256, 18432], P(None, 'col')
- residual: float32 [18432, 18432], P('row', 'col')
All inputs are finite; a program needn't handle non-finite values.
Results may differ from a plain program's by a relative error of at most 0.0003.
Values may be sent and summed in bfloat16 or wider, within the bound.
A program may use at most 128 MiB of HBM per device.

v0:
```python
import jax
import jax.numpy as jnp
from jax import lax
from jax.sharding import PartitionSpec as P

highest = lax.Precision.HIGHEST


def token_product(left_rows, right_rows):
    return lax.dot_general(
        left_rows, right_rows, (((0,), (0,)), ((), ())), preferred_element_type=jnp.float32
    )


def exact_product(left_side, right_side):
    return jnp.dot(left_side, right_side, precision=highest, preferred_element_type=jnp.float32)


def per_device(inputs, out_grads, range_test, corange_test):
    grads_all = lax.all_gather(out_grads, "row", axis=0, tiled=True)
    gradient = token_product(lax.all_gather(inputs, "col", axis=0, tiled=True), grads_all)
    range_sketch = lax.psum(exact_product(gradient, range_test), "col")
    corange_sketch = lax.psum(exact_product(corange_test, gradient), "row")
    core_input = lax.psum(exact_product(corange_test, range_sketch), "row")
    gram_matrix = lax.dot_general(
        core_input,
        core_input,
        (((0,), (0,)), ((), ())),
        precision=highest,
        preferred_element_type=jnp.float32,
    )
    factor_low = jnp.linalg.cholesky(gram_matrix)
    core_map = jax.scipy.linalg.cho_solve((factor_low, True), core_input.T)
    project = exact_product(core_map, corange_sketch)
    residual = gradient - exact_product(range_sketch, project)
    return (range_sketch, corange_sketch, residual)


def solution(mesh):
    placed = (P("col", "row"), P("row", "col"), P("col", None), P(None, "row"))
    return jax.shard_map(
        per_device,
        mesh=mesh,
        in_specs=placed,
        out_specs=(P("row", None), P(None, "col"), P("row", "col")),
        check_vma=False,
    )
```

profile of v0, /device:TPU:1, one launch (start us, length us, event | category | flops | bytes accessed | tf_op | source)
XLA Modules:
  0.0 438.1 jit_solution(6629856623916740087)
XLA Ops:
  7.2 0.0 copy-start
  7.2 0.0 all-gather.3.cloned.1.call-start
  7.2 0.7 all-gather.3.cloned.1.call-update
  7.9 0.0 all-gather.5.cloned.1.call-start
  8.0 0.7 all-gather.5.cloned.1.call-update
  8.7 0.0 copy-start.3
  8.7 0.0 all-reduce.4.cloned.1.call-start
  8.7 86.0 %all-gather.3.cloned.1.call-done = bf16[4096,1152]{1,0:T(8,128)(2,1)} async-done(((bf16[256,1152]{1,0:T(8,128)(2,1)}), bf16[4096,1152]{1,0:T(8,128)(2,1)}) %all-gather.3.cloned.1.call-update) | async-done | bytes 9437200 | tf_op jit(solution)/shard_map/all_gather | solution.py:21
  94.7 63.0 %all-gather.5.cloned.1.call-done = bf16[4096,1152]{1,0:T(8,128)(2,1)} async-done(((bf16[256,1152]{1,0:T(8,128)(2,1)}), bf16[4096,1152]{1,0:T(8,128)(2,1)}) %all-gather.5.cloned.1.call-update) | async-done | bytes 9437200 | tf_op jit(solution)/shard_map/all_gather | solution.py:20
  157.6 17.0 %fusion.6 = f32[1152,1152]{1,0:T(8,128)S(1)} fusion(bf16[4096,1152]{1,0:T(8,128)(2,1)} %all-gather.3.cloned.1.call-done, bf16[4096,1152]{1,0:T(8,128)(2,1)} %all-gather.5.cloned.1.call-done), kind=kOutput, calls=%fused_computation.15 | convolution fusion | flops 10871635968 | bytes 24182784 | tf_op jit(solution)/shard_map/dot_general | solution.py:10
  174.7 0.0 copy-start.1
  174.7 2.4 copy-done.1
  177.1 0.0 copy-done.3
  177.1 5.3 %fusion.7 = f32[1152,128]{1,0:T(8,128)} fusion(f32[1152,1152]{1,0:T(8,128)S(1)} %fusion.6, f32[1152,128]{1,0:T(8,128)S(1)} %copy-done.3), kind=kOutput, calls=%fused_computation.16 | convolution fusion | flops 2038431744 | bytes 6488064 | tf_op jit(solution)/shard_map/dot_general | solution.py:16
  182.4 0.0 all-reduce.4.cloned.1.call-update
  182.4 0.2 all-reduce.6.cloned.1.call-start
  182.6 0.0 copy-done
  182.7 12.0 %convolution_bitcast_fusion = f32[256,1152]{0,1:T(8,128)} fusion(f32[1152,1152]{1,0:T(8,128)} %copy-done.1, f32[256,1152]{1,0:T(8,128)S(1)} %copy-done), kind=kOutput, calls=%fused_computation.1 | convolution fusion | flops 4076863488 | bytes 7667712 | tf_op jit(solution)/shard_map/dot_general | solution.py:16
  194.6 79.5 %all-reduce.4.cloned.1.call-done = f32[1152,128]{1,0:T(8,128)} async-done(((f32[1152,128]{1,0:T(8,128)}), f32[1152,128]{1,0:T(8,128)}) %all-reduce.4.cloned.1.call-update) | async-done | bytes 589840 | tf_op jit(solution)/shard_map/psum | solution.py:22
  274.1 0.0 copy-start.2
  274.1 3.0 convolution_bitcast_fusion.1
  277.1 0.0 all-reduce.6.cloned.1.call-update
  277.1 114.8 %all-reduce.6.cloned.1.call-done = (f32[256,1152]{0,1:T(8,128)}, f32[256,128]{0,1:T(8,128)}) async-done(((f32[256,1152]{0,1:T(8,128)}, f32[256,128]{0,1:T(8,128)}), (f32[256,1152]{0,1:T(8,128)}, f32[256,128]{0,1:T(8,128)})) %all-reduce.6.cloned.1.call-update) | async-done | bytes 1310736 | tf_op jit(solution)/shard_map/psum | solution.py:23
  392.0 1.3 fusion.8
  393.2 0.1 copy.7
  393.3 11.9 %cholesky.16 = f32[128,128]{1,0:T(8,128)S(1)} custom-call(f32[128,128]{1,0:T(8,128)S(1)} %fusion.5), custom_call_target="Cholesky" | custom-call | tf_op jit(solution)/shard_map/jit(cholesky)/cholesky | solution.py:32
  405.3 0.6 compare_reduce_fusion
  405.9 0.7 fusion
  406.6 9.8 %custom-call.10 = f32[1,128,128]{1,2,0:T(8,128)S(1)} custom-call(f32[1,128,128]{2,1,0:T(8,128)S(1)} %fusion), custom_call_target="InvertDiagBlocksLowerTriangular" | custom-call | tf_op jit(solution)/shard_map/jit(_cho_solve)/triangular_solve | solution.py:33
  416.4 1.2 fusion.3
  417.6 0.3 fusion.1
  417.9 2.7 copy.8
  420.6 2.5 fusion.9
  423.0 0.0 copy-done.2
  423.1 7.7 %convolution_subtract_fusion = f32[1152,1152]{1,0:T(8,128)} fusion(f32[1152,1152]{1,0:T(8,128)} %copy-done.1, f32[1152,128]{1,0:T(8,128)S(1)} %copy-done.2, f32[128,1152]{1,0:T(8,128)S(1)} %fusion.9), kind=kOutput, calls=%fused_computation | convolution fusion | flops 2039758848 | bytes 11796480 | tf_op jit(solution)/shard_map/dot_general | solution.py:16
  430.8 0.8 copy.12
  (2 shorter events, 0.0 us)
Async XLA Ops:
  7.2 175.5 %copy-start = (f32[256,1152]{1,0:T(8,128)S(1)}, f32[256,1152]{1,0:T(8,128)}, u32[]{:S(2)}) copy-start(f32[256,1152]{1,0:T(8,128)} %param.7) | copy-start | bytes 3538948
  7.2 87.5 %all-gather.3.cloned.1.call-start = ((), (), s32[]{:S(2)}) async-start(), calls=%async_computation | async-start | bytes 10027008 | tf_op jit(solution)/shard_map/all_gather | solution.py:21
  7.9 149.7 %all-gather.5.cloned.1.call-start = ((), (), s32[]{:S(2)}) async-start(), calls=%async_computation.1 | async-start | bytes 10027008 | tf_op jit(solution)/shard_map/all_gather | solution.py:20
  8.7 168.4 %copy-start.3 = (f32[1152,128]{1,0:T(8,128)S(1)}, f32[1152,128]{1,0:T(8,128)}, u32[]{:S(2)}) copy-start(f32[1152,128]{1,0:T(8,128)} %param.6) | copy-start | bytes 1769476
  8.7 265.4 %all-reduce.4.cloned.1.call-start = ((), (), s32[]{:S(2)}) async-start(), calls=%async_computation.2 | async-start | bytes 1179648 | tf_op jit(solution)/shard_map/psum | solution.py:22
  174.7 2.4 copy-start.1
  182.4 209.6 %all-reduce.6.cloned.1.call-start = ((), (), s32[]{:S(2)}) async-start(), calls=%async_computation.3 | async-start | bytes 2621440 | tf_op jit(solution)/shard_map/psum | solution.py:23
  274.1 149.0 %copy-start.2 = (f32[1152,128]{1,0:T(8,128)S(1)}, f32[1152,128]{1,0:T(8,128)}, u32[]{:S(2)}) copy-start(f32[1152,128]{1,0:T(8,128)} %all-reduce.4.cloned.1.call-done) | copy-start | bytes 1769476
Sparse Core Ops, SparseCore 0:
  10.5 84.1 all-gather.2
  96.5 61.0 all-gather.4
  182.5 91.4 all-reduce.3
  277.3 114.6 all-reduce.5
where the time goes:
time: 438 us
  waiting for transfers between devices  345 us (79%)
  matrix products  50.3 us (11%)
  other arithmetic  23.1 us (5%)
  between operations  13.9 us (3%)
  local copies, waits for them, and re-layouts  5.95 us (1%)
    psum x1, waiting for transfers between devices, per_device(): corange_sketch = lax.psum(exact_product(corange_test, gradient), 'row')  115 us
    all_gather x1, waiting for transfers between devices, per_device(): lax.all_gather(inputs, 'col', axis=0, tiled=True)  86 us
    psum x1, waiting for transfers between devices, per_device(): range_sketch = lax.psum(exact_product(gradient, range_test), 'col')  79.5 us
    all_gather x1, waiting for transfers between devices, per_device(): grads_all = lax.all_gather(out_grads, 'row', axis=0, tiled=True)  63 us
    dot_general x5, matrix products, exact_product(): jnp.dot(left_side, right_side, precision=highest, preferred_element_type=...  30.5 us
    dot_general x1, matrix products, token_product(): lax.dot_general(left_rows, right_rows, (((0,), (0,)), ((), ())), preferre...  17 us
    another operation x3, other arithmetic, per_device(): factor_low = jnp.linalg.cholesky(gram_matrix)  12.6 us
    another operation x2, other arithmetic, per_device(): core_map = jax.scipy.linalg.cho_solve((factor_low, True), core_input.T)  10.5 us
  transfers between devices with their start and end apart: 4, of which 4 were waited for; matrix products, arithmetic and copies ran while one was open for 3% of the time, Pallas kernels for 0%

commit v1 on v0

v1 whole, which is shorter than its diff:
```python
import jax
import jax.numpy as jnp
from jax import lax
from jax.experimental import pallas as pl
from jax.experimental.pallas import tpu as pltpu
from jax.sharding import PartitionSpec as P

F32 = jnp.float32
BF16 = jnp.bfloat16
HIGHEST = lax.Precision.HIGHEST
MESH = pl.DeviceIdType.MESH

BLOCK = 1152
TOK = 256
UNIT = 288
COLS = 384
RY = 128
RZ = 256


def dot(left_side, right_side, precision=None):
    return jnp.dot(left_side, right_side, precision=precision, preferred_element_type=F32)


def split(value, parts):
    out = []
    for _ in range(parts):
        piece = value.astype(BF16)
        value = value - piece.astype(F32)
        out.append(piece)
    return out


def exchange_kernel(
    xt_ref, y_ref, om_ref, psi_ref,
    q_ref, p_ref, r_ref, g_hbm,
    xt4, yf, af, wf, ahl, whl, g_acc, a_part, w_part, a_in, w_in, inv_ref,
    rs_send, rs_recv, ag_send, ag_recv, ring_send, ring_recv, prt_send, prt_recv,
    z_send, z_recv, yp_send, yp_recv, own_send, own_recv, local_sem, g_sem,
):
    row, col = lax.axis_index("row"), lax.axis_index("col")
    z, k = row // 2, row % 2
    x, y = col // 4, col % 4
    partner = row + 1 - 2 * k

    barrier = pltpu.get_barrier_semaphore()

    def greet(j, carry):
        pl.semaphore_signal(barrier, inc=1, device_id=((row + j) % 16, col), device_id_type=MESH)
        pl.semaphore_signal(barrier, inc=1, device_id=(row, (col + j) % 16), device_id_type=MESH)
        return carry

    lax.fori_loop(1, 16, greet, 0)

    def own_left(i, carry):
        rows = pl.ds(pl.multiple_of(i * 128, 128), 128)
        parts = jnp.concatenate(split(psi_ref[rows, :], 3), axis=0)
        both = dot(parts, xt_ref[...])
        total = both[0:128] + both[128:256] + both[256:384]
        a_part[pl.ds(pl.multiple_of(i * 8, 8), 8)] = total.reshape(8, 16, TOK)
        return carry

    lax.fori_loop(0, 2, own_left, 0)
    parts = jnp.concatenate(split(om_ref[...], 3), axis=1)
    both = dot(y_ref[...], parts)
    w_part[...] = (both[:, 0:128] + both[:, 128:256] + both[:, 256:384]).reshape(16, 16, RY)

    pl.semaphore_wait(barrier, 30)

    def remote(source, target, send, recv, device):
        return pltpu.make_async_remote_copy(
            src_ref=source, dst_ref=target, send_sem=send, recv_sem=recv,
            device_id=device, device_id_type=MESH,
        )

    me_row = 8 * k + z

    def rs_left(t):
        slot = 8 * (t % 2) + t // 2
        return remote(a_part.at[slot], a_in.at[me_row], rs_send.at[0, slot], rs_recv.at[0, me_row], (t, col))

    def rs_right(t):
        return remote(w_part.at[t], w_in.at[col], rs_send.at[1, t], rs_recv.at[1, col], (row, t))

    def rs_start(j, carry):
        rs_left((row + j) % 16).start()
        rs_right((col + j) % 16).start()
        return carry

    lax.fori_loop(1, 16, rs_start, 0)

    def view(p, v, first, second):
        xi, yi = (first, second) if v < 2 else (second, first)
        if p == 0:
            return xt4.at[xi, yi, pl.ds(UNIT * v, UNIT), :]
        if p == 1:
            return af.at[xi, yi, k, pl.ds(2 * v, 2)]
        return wf.at[xi, yi, k, pl.ds(2 * v, 2)]

    def axes(v):
        return (x, y) if v < 2 else (y, x)

    def neighbour(v, phase, step):
        along_x = (v < 2) == (phase == 0)
        if along_x:
            return (row, ((x + step + 4) % 4) * 4 + y)
        return (row, x * 4 + (y + step + 4) % 4)

    def ring_view(p, v, phase, offset):
        first, second = axes(v)
        if phase == 0:
            return view(p, v, (first + offset + 4) % 4, second)
        return view(p, v, slice(None), (second + offset + 4) % 4)

    def ring_send_copy(p, v, phase, j):
        far = 1 if v % 2 == 0 else -1
        step = (1, -1, far)[j]
        offset = (0, 0, -far)[j]
        here = ring_view(p, v, phase, offset)
        return remote(
            here, here, ring_send.at[p, v, phase, j], ring_recv.at[p, v, phase, j], neighbour(v, phase, step)
        )

    def ring_start(p, v, phase):
        ring_send_copy(p, v, phase, 0).start()
        ring_send_copy(p, v, phase, 1).start()

    def ring_wait(p, v, phase, j):
        there = ring_view(p, v, phase, (-1, 1, 2)[j])
        remote(
            there, there, ring_send.at[p, v, phase, j], ring_recv.at[p, v, phase, j], neighbour(v, phase, 1)
        ).wait_recv()

    def partner_copy(p, v, phase, j):
        there = ring_view(p, v, phase, (-1, 1, 2)[j])
        return remote(
            there, there, prt_send.at[p, v, phase, j], prt_recv.at[p, v, phase, j], (partner, col)
        )

    def ring_near(p, v, phase):
        far = 0 if v % 2 == 0 else 1
        for j in (far, 1 - far):
            ring_wait(p, v, phase, j)
            if j == far:
                ring_send_copy(p, v, phase, 2).start()
            if p:
                partner_copy(p, v, phase, j).start()

    def ring_far(p, v, phase):
        ring_wait(p, v, phase, 2)
        if p:
            partner_copy(p, v, phase, 2).start()

    def z_view(h, offset):
        return yf.at[2 * ((z + offset + 8) % 8) + k, :, pl.ds(COLS * h, COLS)]

    def z_copy(h, d, s):
        step = 1 if d == 0 else -1
        here = z_view(h, -s * step)
        return remote(here, here, z_send.at[h, d, s], z_recv.at[h, d, s], (2 * ((z + step + 8) % 8) + k, col))

    def z_long(h, d):
        return (h % 2) == d

    def yp_copy(h, d, s):
        here = z_view(h, -s if d == 0 else s)
        return remote(here, here, yp_send.at[h, d, s], yp_recv.at[h, d, s], (partner, col))

    def z_own(h):
        z_copy(h, 0, 0).start()
        z_copy(h, 1, 0).start()
        yp_copy(h, 0, 0).start()

    def z_event(h, s):
        for d in (0, 1):
            if s == 4 and not z_long(h, d):
                continue
            step = 1 if d == 0 else -1
            here = z_view(h, -s * step)
            remote(here, here, z_send.at[h, d, s - 1], z_recv.at[h, d, s - 1], (partner, col)).wait_recv()
            if s < 3 or (s == 3 and z_long(h, d)):
                z_copy(h, d, s).start()
            yp_copy(h, d, s).start()

    own_x = pltpu.make_async_copy(xt_ref, xt4.at[x, y], local_sem.at[0])
    own_y = pltpu.make_async_copy(y_ref, yf.at[row], local_sem.at[1])
    own_x.start()
    own_y.start()
    own_x.wait()
    own_y.wait()
    for v in range(4):
        ring_start(0, v, 0)
    z_own(0)

    def rs_done(j, carry):
        t, c = (row + j) % 16, (col + j) % 16
        slot = 8 * (t % 2) + t // 2
        remote(a_part.at[slot], a_in.at[slot], rs_send.at[0, slot], rs_recv.at[0, slot], (t, col)).wait()
        remote(w_part.at[c], w_in.at[c], rs_send.at[1, c], rs_recv.at[1, c], (row, c)).wait()
        return carry

    lax.fori_loop(1, 16, rs_done, 0)

    def rs_sum(j, carry):
        left, right = carry
        t, c = (row + j) % 16, (col + j) % 16
        slot = 8 * (t % 2) + t // 2
        return left + a_in[slot], right + w_in[c]

    left, right = lax.fori_loop(1, 16, rs_sum, (a_part[me_row], w_part[col]))
    af[x, y, k, z] = left
    wf[x, y, k, z] = right
    z_own(1)

    def ag_copy(p, t):
        here = af.at[x, y, k, z] if p == 0 else wf.at[x, y, k, z]
        return remote(here, here, ag_send.at[p, t], ag_recv.at[p, z], (2 * t + k, col))

    def ag_start(j, carry):
        t = (z + j) % 8
        ag_copy(0, t).start()
        ag_copy(1, t).start()
        return carry

    lax.fori_loop(1, 8, ag_start, 0)

    for v in (0, 2, 1, 3):
        ring_near(0, v, 0)
    z_event(0, 1)
    for v in (0, 2):
        ring_far(0, v, 0)
        ring_start(0, v, 1)

    def ag_done(j, carry):
        t = (z + j) % 8
        for p, buffer in enumerate((af, wf)):
            there = buffer.at[x, y, k, t]
            remote(there, there, ag_send.at[p, t], ag_recv.at[p, t], (2 * t + k, col)).wait_recv()
        return carry

    lax.fori_loop(1, 8, ag_done, 0)
    for v in range(4):
        for p in (1, 2):
            ring_start(p, v, 0)
    own_half = []
    for p, buffer in enumerate((af, wf)):
        half = buffer.at[x, y, k]
        copy = remote(half, half, own_send.at[p], own_recv.at[p], (partner, col))
        copy.start()
        own_half.append(copy)

    z_event(1, 1)
    z_event(0, 2)
    for v in range(4):
        for p in (1, 2):
            ring_near(p, v, 0)
    z_event(1, 2)
    z_own(2)
    for v in range(4):
        for p in (1, 2):
            ring_far(p, v, 0)
            ring_start(p, v, 1)
    for v in (1, 3):
        ring_far(0, v, 0)
    for v in (0, 2):
        ring_near(0, v, 1)
    z_event(0, 3)
    for v in (1, 3):
        ring_start(0, v, 1)
    z_event(1, 3)
    for v in range(4):
        for p in (1, 2):
            ring_near(p, v, 1)
    z_event(0, 4)
    z_event(1, 4)
    for v in range(4):
        for p in (1, 2):
            ring_far(p, v, 1)
    z_event(2, 1)

    for p, buffer in enumerate((af, wf)):
        half = buffer.at[x, y, 1 - k]
        remote(half, half, own_send.at[p], own_recv.at[p], (partner, col)).wait_recv()
    for p in (1, 2):
        buffer = (af, wf)[p - 1]
        for v in range(4):
            first, second = axes(v)
            for phase in (0, 1):
                for j in range(3):
                    offset = (-1, 1, 2)[j]
                    if phase == 0:
                        f, s = (first + offset + 4) % 4, second
                    else:
                        f, s = slice(None), (second + offset + 4) % 4
                    xi, yi = (f, s) if v < 2 else (s, f)
                    there = buffer.at[xi, yi, 1 - k, pl.ds(2 * v, 2)]
                    remote(
                        there, there, prt_send.at[p, v, phase, j], prt_recv.at[p, v, phase, j], (partner, col)
                    ).wait_recv()

    z_event(2, 2)

    def core_step(b, core):
        left = af[b // 4, b % 4].reshape(RZ, TOK)
        right = wf[:, :, b % 2, b // 2].reshape(TOK, RY)
        ahl[b] = jnp.concatenate(split(left, 2), axis=0)
        whl[b] = jnp.concatenate(split(right, 2), axis=1)
        return core + dot(left, right, HIGHEST)

    core = lax.fori_loop(0, 16, core_step, jnp.zeros((RZ, RY), F32))
    z_event(2, 3)
    core_t = core.T
    inv_ref[...] = dot(core_t, core, HIGHEST)
    lanes = lax.broadcasted_iota(jnp.int32, (RY, RY), 1)
    subs = lax.broadcasted_iota(jnp.int32, (RY, RY), 0)

    def pivot(i, carry):
        now = inv_ref[...]
        line = inv_ref[pl.ds(i, 1), :]
        at_lane = lanes == i
        across = jnp.sum(jnp.where(at_lane, now, 0.0), axis=1, keepdims=True)
        head = jnp.sum(jnp.where(at_lane[0:1], line, 0.0), axis=1, keepdims=True)
        scaled = line / head
        inner = now - across * scaled
        on_line = jnp.where(at_lane, 1.0 / head, scaled)
        off_line = jnp.where(at_lane, -across / head, inner)
        inv_ref[...] = jnp.where(subs == i, on_line, off_line)
        return carry

    lax.fori_loop(0, RY, pivot, 0)
    core_map = dot(inv_ref[...], core_t, HIGHEST)

    z_event(2, 4)
    for v in (1, 3):
        ring_near(0, v, 1)
    for v in (0, 2, 1, 3):
        ring_far(0, v, 1)

    for h in range(3):
        for d in (0, 1):
            for s in range(5):
                if (s == 0 and d == 1) or (s == 4 and not z_long(h, d)):
                    continue
                offset = -s if d == 0 else s
                there = yf.at[2 * ((z + offset + 8) % 8) + 1 - k, :, pl.ds(COLS * h, COLS)]
                remote(there, there, yp_send.at[h, d, s], yp_recv.at[h, d, s], (partner, col)).wait_recv()

    def unit_rows(u):
        rows = pl.ds(pl.multiple_of(u * UNIT, 32), UNIT)
        return jnp.concatenate([xt4[b // 4, b % 4, rows, :] for b in range(16)], axis=1)

    def right_step(u, carry):
        rows = pl.ds(pl.multiple_of(u * UNIT, 32), UNIT)
        both = dot(unit_rows(u), whl[...].reshape(16 * TOK, 2 * RY))
        q_ref[rows, :] = both[:, 0:RY] + both[:, RY:]
        return carry

    lax.fori_loop(0, 4, right_step, 0)

    def left_step(h, carry):
        cols = pl.ds(pl.multiple_of(h * COLS, 128), COLS)
        lhs = jnp.concatenate([ahl[b] for b in range(16)], axis=1)
        both = dot(lhs, yf[:, :, cols].reshape(16 * TOK, COLS))
        total = both[0:RZ] + both[RZ:]
        p_ref[:, cols] = total
        r_ref[:, cols] = dot(core_map, total, HIGHEST)
        return carry

    lax.fori_loop(0, 3, left_step, 0)

    def tile_step(i, carry):
        u, h = i // 3, i % 3
        rows = pl.ds(pl.multiple_of(u * UNIT, 32), UNIT)
        cols = pl.ds(pl.multiple_of(h * COLS, 128), COLS)
        g_acc[rows, cols] = dot(unit_rows(u), yf[:, :, cols].reshape(16 * TOK, COLS))
        return carry

    lax.fori_loop(0, 12, tile_step, 0)
    out = pltpu.make_async_copy(g_acc, g_hbm, g_sem)
    out.start()

    def ag_sent(j, carry):
        t = (z + j) % 8
        ag_copy(0, t).wait_send()
        ag_copy(1, t).wait_send()
        return carry

    lax.fori_loop(1, 8, ag_sent, 0)
    for copy in own_half:
        copy.wait_send()
    for v in range(4):
        for phase in (0, 1):
            for j in range(3):
                for p in range(3):
                    ring_send_copy(p, v, phase, j).wait_send()
                    if p:
                        partner_copy(p, v, phase, j).wait_send()
    for h in range(3):
        for d in (0, 1):
            for s in range(5):
                if s < 3 or (s == 3 and z_long(h, d)):
                    z_copy(h, d, s).wait_send()
                if (s == 0 and d == 1) or (s == 4 and not z_long(h, d)):
                    continue
                yp_copy(h, d, s).wait_send()
    out.wait()


def exchange(xt, y, om, psi):
    dma = pltpu.SemaphoreType.DMA
    return pl.pallas_call(
        exchange_kernel,
        name="exchange",
        out_shape=(
            jax.ShapeDtypeStruct((BLOCK, RY), F32),
            jax.ShapeDtypeStruct((RZ, BLOCK), F32),
            jax.ShapeDtypeStruct((RY, BLOCK), F32),
            jax.ShapeDtypeStruct((BLOCK, BLOCK), F32),
        ),
        in_specs=[pl.BlockSpec(memory_space=pltpu.VMEM)] * 4,
        out_specs=(
            pl.BlockSpec(memory_space=pltpu.VMEM),
            pl.BlockSpec(memory_space=pltpu.VMEM),
            pl.BlockSpec(memory_space=pltpu.VMEM),
            pl.BlockSpec(memory_space=pl.ANY),
        ),
        scratch_shapes=[
            pltpu.VMEM((4, 4, BLOCK, TOK), BF16),
            pltpu.VMEM((16, TOK, BLOCK), BF16),
            pltpu.VMEM((4, 4, 2, 8, 16, TOK), F32),
            pltpu.VMEM((4, 4, 2, 8, 16, RY), F32),
            pltpu.VMEM((16, 2 * RZ, TOK), BF16),
            pltpu.VMEM((16, TOK, 2 * RY), BF16),
            pltpu.VMEM((BLOCK, BLOCK), F32),
            pltpu.VMEM((16, 16, TOK), F32),
            pltpu.VMEM((16, 16, RY), F32),
            pltpu.VMEM((16, 16, TOK), F32),
            pltpu.VMEM((16, 16, RY), F32),
            pltpu.VMEM((RY, RY), F32),
            dma((2, 16)), dma((2, 16)),
            dma((2, 8)), dma((2, 8)),
            dma((3, 4, 2, 3)), dma((3, 4, 2, 3)),
            dma((3, 4, 2, 3)), dma((3, 4, 2, 3)),
            dma((3, 2, 4)), dma((3, 2, 4)),
            dma((3, 2, 5)), dma((3, 2, 5)),
            dma((2,)), dma((2,)),
            dma((2,)), dma,
        ],
        compiler_params=pltpu.CompilerParams(
            collective_id=0, has_side_effects=True, vmem_limit_bytes=62 * 1024 * 1024
        ),
    )(xt, y, om, psi)


def finish_kernel(g_ref, q_ref, r_ref, p_ref, res_ref, qo_ref, po_ref):
    q_high, q_low = split(q_ref[...], 2)
    r_high, r_low = split(r_ref[...], 2)
    left = jnp.concatenate([q_high, q_low, q_high], axis=1)
    right = jnp.concatenate([r_high, r_high, r_low], axis=0)
    res_ref[...] = g_ref[...] - dot(left, right)
    qo_ref[...] = q_ref[...]
    po_ref[...] = p_ref[...]


def finish(g, q, r, p):
    steps = 8
    rows, prows = BLOCK // steps, RZ // steps
    return pl.pallas_call(
        finish_kernel,
        name="finish",
        grid=(steps,),
        out_shape=(
            jax.ShapeDtypeStruct((BLOCK, BLOCK), F32),
            jax.ShapeDtypeStruct((BLOCK, RY), F32),
            jax.ShapeDtypeStruct((RZ, BLOCK), F32),
        ),
        in_specs=[
            pl.BlockSpec((rows, BLOCK), lambda i: (i, 0)),
            pl.BlockSpec((rows, RY), lambda i: (i, 0)),
            pl.BlockSpec((RY, BLOCK), lambda i: (0, 0)),
            pl.BlockSpec((prows, BLOCK), lambda i: (i, 0)),
        ],
        out_specs=(
            pl.BlockSpec((rows, BLOCK), lambda i: (i, 0)),
            pl.BlockSpec((rows, RY), lambda i: (i, 0)),
            pl.BlockSpec((prows, BLOCK), lambda i: (i, 0)),
        ),
    )(g, q, r, p)


def per_device(inputs, out_grads, range_test, corange_test):
    q, p, r, g = exchange(inputs.T, out_grads, range_test, corange_test)
    residual, q, p = finish(g, q, r, p)
    return (q, p, residual)


def solution(mesh):
    placed = (P("col", "row"), P("row", "col"), P("col", None), P(None, "row"))
    return jax.shard_map(
        per_device,
        mesh=mesh,
        in_specs=placed,
        out_specs=(P("row", None), P(None, "col"), P("row", "col")),
        check_vma=False,
    )
```

time: 438 us -> 171 us (0.39)
  waiting for transfers between devices: 345 us -> 0 us
  Pallas kernels: 0 us -> 165 us
  matrix products: 50.3 us -> 0 us
  other arithmetic: 23.1 us -> 0 us
  between operations: 13.9 us -> 0.64 us
    psum x2 -> x0, waiting for transfers between devices: 194 us -> none  [the longest x1 115 us: per_device(): corange_sketch = lax.psum(exact_product(corange_test, gradient), 'row')]
    pallas_call x0 -> x2, Pallas kernels: none -> 165 us  [the longest x1 156 us: exchange(): pl.pallas_call(exchange_kernel, name='exchange', out_shape=(jax.ShapeDtyp...]
    all_gather x2 -> x0, waiting for transfers between devices: 149 us -> none  [the longest x1 86 us: per_device(): lax.all_gather(inputs, 'col', axis=0, tiled=True)]
    dot_general x7 -> x0, matrix products: 48.8 us -> none  [the longest x5 30.5 us: exact_product(): jnp.dot(left_side, right_side, precision=highest, preferred_element_type=...]
    another operation x5 -> x0, other arithmetic: 23.1 us -> none  [the longest x3 12.6 us: per_device(): factor_low = jnp.linalg.cholesky(gram_matrix)]
  transfers between devices with their start and end apart: 4 -> 0, of which waited for: 4 -> 0; matrix products, arithmetic and copies ran while one was open for 3% -> 0% of each run, Pallas kernels for 0% -> 0%
where the time goes in v1:
time: 171 us; the launch traced here: 168 us
  Pallas kernels  165 us (96%)
  local copies, waits for them, and re-layouts  2.12 us (1%)
    pallas_call x1, Pallas kernels, exchange(): pl.pallas_call(exchange_kernel, name='exchange', out_shape=(jax.ShapeDtyp...  156 us
    pallas_call x1, Pallas kernels, finish(): pl.pallas_call(finish_kernel, name='finish', grid=(steps,), out_shape=(ja...  9.31 us

profile of v1, /device:TPU:1, one launch (start us, length us, event | category | flops | bytes accessed | tf_op | source)
XLA Modules:
  0.0 168.0 jit_solution(13715661158456584470)
XLA Ops:
  0.6 2.1 %copy.7 = bf16[256,1152]{0,1:T(8,128)(2,1)} copy(bf16[256,1152]{1,0:T(8,128)(2,1)} %param.4) | data formatting | bytes 1179648 | tf_op args[0]
  2.7 155.9 %exchange.1 = (f32[1152,128]{1,0:T(8,128)}, f32[256,1152]{1,0:T(8,128)}, f32[128,1152]{1,0:T(8,128)}, f32[1152,1152]{1,0:T(8,128)}) custom-call(bf16[1152,256]{1,0:T(8,128)(2,1)} %bitcast.1, bf16[256,1152]{1,0:T(8,128)(2,1)} %y_ref.1, f32[1152,128]{1,0:T(8,128)} %om_ref.1, f32[256,1152]{1,0:T(8,128)} %psi_ref.1), custom_call_target="tpu_custom_call" | custom-call | tf_op jit(solution)/shard_map/exchange/pallas_call | solution.py:411
  158.7 9.3 %finish.1 = (f32[1152,1152]{1,0:T(8,128)}, f32[1152,128]{1,0:T(8,128)}, f32[256,1152]{1,0:T(8,128)}) custom-call(f32[1152,1152]{1,0:T(8,128)} %get-tuple-element.10.g_ref, f32[1152,128]{1,0:T(8,128)} %get-tuple-element.11.q_ref, f32[128,1152]{1,0:T(8,128)} %get-tuple-element.12.r_ref, f32[256,1152]{1,0:T(8,128)} %get-tuple-element.13.p_ref), custom_call_target="tpu_custom_call" | custom-call | tf_op jit(solution)/shard_map/finish/pallas_call | solution.py:468

commit v2 on v0

v2 whole, which is shorter than its diff:
```python
import heapq

import jax
import jax.numpy as jnp
from jax import lax
from jax.experimental import pallas as pl
from jax.experimental.pallas import tpu as pltpu
from jax.sharding import PartitionSpec as P

F32 = jnp.float32
BF16 = jnp.bfloat16
HIGHEST = lax.Precision.HIGHEST
MESH = pl.DeviceIdType.MESH

BLOCK = 1152
TOK = 256
RY = 128
RZ = 256
UNITS = (384, 384, 256, 128)
CHUNKS = (512, 512, 128)
FINISH_COLS = 384

LINK_RATE = 46500.0
PARTNER_RATE = 150000.0
HOP = 1.6
SLACK = 2.5


def starts(sizes):
    return [sum(sizes[:i]) for i in range(len(sizes))]


UNIT_AT = starts(UNITS)
CHUNK_AT = starts(CHUNKS)


def dot(left_side, right_side, precision=None):
    return jnp.dot(left_side, right_side, precision=precision, preferred_element_type=F32)


def split(value, parts):
    out = []
    for _ in range(parts):
        piece = value.astype(BF16)
        value = value - piece.astype(F32)
        out.append(piece)
    return out


class Message:
    def __init__(self, name, loads, order, start, wait, then=None, sent=None, latency=HOP):
        self.name, self.loads, self.order = name, loads, order
        self.start, self.wait, self.then, self.sent, self.latency = start, wait, then, sent, latency


class Plan:
    def __init__(self):
        self.now, self.free, self.queues = 0.0, {}, {}
        self.flying, self.count, self.done, self.tasks, self.sent = [], 0, set(), [], []

    def post(self, message):
        self.count += 1
        link = next(iter(message.loads))
        heapq.heappush(self.queues.setdefault(link, []), (message.order, self.count, message))

    def launch(self, message):
        message.start()
        self.now += 0.03
        end = self.now
        for link, cost in message.loads.items():
            self.free[link] = max(self.now, self.free.get(link, 0.0)) + cost
            end = max(end, self.free[link])
        self.count += 1
        heapq.heappush(self.flying, (end + message.latency, self.count, message))
        if message.sent:
            self.sent.append(message.sent)

    def poll(self):
        for link, queue in self.queues.items():
            while queue and self.free.get(link, 0.0) - self.now < SLACK:
                self.launch(heapq.heappop(queue)[2])

    def task(self, name, needs, order, cost, run):
        self.tasks.append((order, len(self.tasks), name, frozenset(needs), cost, run))

    def finish(self, name):
        self.done.add(name)

    def run(self, log=None):
        while True:
            self.poll()
            if self.flying and self.flying[0][0] <= self.now:
                message = heapq.heappop(self.flying)[2]
                message.wait()
                if log is not None:
                    log.append((round(self.now, 1), "recv", message.name))
                self.now += 0.03
                self.finish(message.name)
                if message.then:
                    message.then()
                continue
            ready = [task for task in self.tasks if task[3] <= self.done]
            if ready:
                best = min(ready)
                self.tasks.remove(best)
                if log is not None:
                    log.append((round(self.now, 1), "task", best[2]))
                best[5]()
                self.now += best[4]
                self.finish(best[2])
                continue
            if not self.flying:
                break
            self.now = self.flying[0][0]
        assert not self.tasks, [(task[2], task[3] - self.done) for task in self.tasks]


def exchange_kernel(
    x_hbm, y_hbm, om_hbm, psi_hbm,
    q_ref, r_ref, p_hbm, g_hbm,
    xt4, yf, wf, ar, ahl, whl, g_acc, p_all, c_all, map_ref,
    x_own, om, psi, a_part, w_part, a_in, w_in, inv_ref,
    rs_send, rs_recv, ga_send, ga_recv, gw_send, gw_recv, gc_send, gc_recv, gp_send, gp_recv,
    x_send, x_recv, w_send, w_recv, wp_send, wp_recv,
    z_send, z_recv, yp_send, yp_recv, p_send, p_recv, pp_send, pp_recv,
    own_send, own_recv, local_sem, out_sem,
):
    row, col = lax.axis_index("row"), lax.axis_index("col")
    z, k = row // 2, row % 2
    x, y = col // 4, col % 4
    partner = row + 1 - 2 * k
    me_row = 8 * k + z

    loads_in = [
        pltpu.make_async_copy(x_hbm, x_own, local_sem.at[0]),
        pltpu.make_async_copy(y_hbm, yf.at[row], local_sem.at[1]),
        pltpu.make_async_copy(psi_hbm, psi, local_sem.at[2]),
        pltpu.make_async_copy(om_hbm, om, local_sem.at[3]),
    ]
    for copy in loads_in:
        copy.start()

    barrier = pltpu.get_barrier_semaphore()

    def greet(j, carry):
        pl.semaphore_signal(barrier, inc=1, device_id=((row + j) % 16, col), device_id_type=MESH)
        pl.semaphore_signal(barrier, inc=1, device_id=(row, (col + j) % 16), device_id_type=MESH)
        return carry

    lax.fori_loop(1, 16, greet, 0)

    def remote(source, target, send, recv, device):
        return pltpu.make_async_remote_copy(
            src_ref=source, dst_ref=target, send_sem=send, recv_sem=recv,
            device_id=device, device_id_type=MESH,
        )

    plan = Plan()

    def along(first_axis, step):
        if first_axis:
            return (row, ((x + step + 4) % 4) * 4 + y)
        return (row, x * 4 + (y + step + 4) % 4)

    def x_view(u, a, o1, o2):
        n = UNITS[u] // 2
        rows = pl.ds(UNIT_AT[u] + n * a, n)
        ox, oy = (o1, o2) if a == 0 else (o2, o1)
        return xt4.at[(x + ox + 4) % 4, (y + oy + 4) % 4, rows, :]

    def x_message(u, a, phase, o1, step, hop):
        on_x = (a == 0) == (phase == 0)
        link = ("x" if on_x else "y") + ("+" if step > 0 else "-")
        if phase == 0:
            slot = {(1, 1): 0, (-1, 1): 1}.get((step, hop), 2)
            out_o, in_o = (-step * (hop - 1), 0), (-step * hop, 0)
        else:
            slot = 3 + 3 * (o1 % 4) + {(1, 1): 0, (-1, 1): 1}.get((step, hop), 2)
            out_o, in_o = (o1, -step * (hop - 1)), (o1, -step * hop)
        here, there = x_view(u, a, *out_o), x_view(u, a, *in_o)
        send, recv = x_send.at[u, a, slot], x_recv.at[u, a, slot]
        name = ("x", u, a, slot)

        def start():
            remote(here, here, send, recv, along(on_x, step)).start()

        def wait():
            remote(there, there, send, recv, along(on_x, step)).wait_recv()

        def sent():
            remote(here, here, send, recv, along(on_x, step)).wait_send()

        def then():
            if phase == 0:
                far = 1 if (u + a) % 2 == 0 else -1
                if hop == 1 and step == far:
                    plan.post(x_message(u, a, 0, 0, step, 2))
                came = (-step * hop) % 4
                plan.post(x_message(u, a, 1, came, 1, 1))
                plan.post(x_message(u, a, 1, came, -1, 1))
            else:
                far = 1 if (o1 % 4 in (0, 2)) == ((u + a) % 2 == 0) else -1
                if hop == 1 and step == far:
                    plan.post(x_message(u, a, 1, o1, step, 2))

        cost = UNITS[u] // 2 * TOK * 2 / LINK_RATE
        return Message(name, {link: cost}, (1, u, phase), start, wait, then, sent)

    def x_names(u):
        return [("x", u, a, slot) for a in (0, 1) for slot in range(15)]

    def x_begin(u):
        for a in (0, 1):
            for phase in (0, 1):
                for step in (1, -1):
                    plan.post(x_message(u, a, phase, 0, step, 1))

    def ring_long(h, d):
        return (h % 2) == d

    def z_peer(step):
        return (2 * ((z + step + 8) % 8) + k, col)

    def y_view(h, offset, kk):
        return yf.at[2 * ((z + offset + 8) % 8) + kk, :, pl.ds(CHUNK_AT[h], CHUNKS[h])]

    def p_view(h, offset, kk):
        return p_all.at[kk, (z + offset + 8) % 8, :, pl.ds(CHUNK_AT[h], CHUNKS[h])]

    kinds = {
        "y": (y_view, z_send, z_recv, yp_send, yp_recv, TOK * 2, 1),
        "p": (p_view, p_send, p_recv, pp_send, pp_recv, 64, 0),
    }

    def partner_message(kind, h, d, s):
        view, _, _, send_sem, recv_sem, height, order = kinds[kind]
        offset = -s if d == 0 else s
        here, there = view(h, offset, k), view(h, offset, 1 - k)
        send, recv = send_sem.at[h, d, s], recv_sem.at[h, d, s]

        def start():
            remote(here, here, send, recv, (partner, col)).start()

        def wait():
            remote(there, there, send, recv, (partner, col)).wait_recv()

        def sent():
            remote(here, here, send, recv, (partner, col)).wait_send()

        cost = CHUNKS[h] * height / PARTNER_RATE
        return Message((kind + "p", h, d, s), {"p": cost}, (order, h), start, wait, None, sent)

    def ring_message(kind, h, d, s):
        view, send_sem, recv_sem, _, _, height, order = kinds[kind]
        step = 1 if d == 0 else -1
        here, there = view(h, -step * (s - 1), k), view(h, -step * s, k)
        send, recv = send_sem.at[h, d, s - 1], recv_sem.at[h, d, s - 1]

        def start():
            remote(here, here, send, recv, z_peer(step)).start()

        def wait():
            remote(there, there, send, recv, z_peer(step)).wait_recv()

        def sent():
            remote(here, here, send, recv, z_peer(step)).wait_send()

        def then():
            if s < 3 or (s == 3 and ring_long(h, d)):
                plan.post(ring_message(kind, h, d, s + 1))
            plan.post(partner_message(kind, h, d, s))

        cost = CHUNKS[h] * height / LINK_RATE
        return Message((kind, h, d, s), {"z+" if d == 0 else "z-": cost}, (order, h, s), start, wait, then, sent)

    def ring_begin(kind, h):
        plan.post(ring_message(kind, h, 0, 1))
        plan.post(ring_message(kind, h, 1, 1))
        plan.post(partner_message(kind, h, 0, 0))

    def ring_names(kind, h):
        names = [(kind + "p", h, 0, 0)]
        for d in (0, 1):
            for s in (1, 2, 3) + ((4,) if ring_long(h, d) else ()):
                names += [(kind, h, d, s), (kind + "p", h, d, s)]
        return names

    def w_view(v, phase, offset, kk):
        first, second = (x, y) if v < 2 else (y, x)
        if phase == 0:
            f, s = (first + offset + 4) % 4, second
        else:
            f, s = slice(None), (second + offset + 4) % 4
        xi, yi = (f, s) if v < 2 else (s, f)
        return wf.at[xi, yi, kk, pl.ds(2 * v, 2)]

    def w_partner(v, phase, j):
        offset = (-1, 1, 2)[j]
        here, there = w_view(v, phase, offset, k), w_view(v, phase, offset, 1 - k)
        send, recv = wp_send.at[v, phase, j], wp_recv.at[v, phase, j]

        def start():
            remote(here, here, send, recv, (partner, col)).start()

        def wait():
            remote(there, there, send, recv, (partner, col)).wait_recv()

        def sent():
            remote(here, here, send, recv, (partner, col)).wait_send()

        cost = 16384 * (4 if phase else 1) / PARTNER_RATE
        return Message(("wp", v, phase, j), {"p": cost}, (0,), start, wait, None, sent)

    def w_message(v, phase, j):
        far = 1 if v % 2 == 0 else -1
        step = (1, -1, far)[j]
        here, there = w_view(v, phase, (0, 0, -far)[j], k), w_view(v, phase, (-1, 1, 2)[j], k)
        send, recv = w_send.at[v, phase, j], w_recv.at[v, phase, j]
        on_x = (v < 2) == (phase == 0)
        link = ("x" if on_x else "y") + ("+" if step > 0 else "-")

        def start():
            remote(here, here, send, recv, along(on_x, step)).start()

        def wait():
            remote(there, there, send, recv, along(on_x, step)).wait_recv()

        def sent():
            remote(here, here, send, recv, along(on_x, step)).wait_send()

        def then():
            if j < 2 and step == far:
                plan.post(w_message(v, phase, 2))
            plan.post(w_partner(v, phase, j))

        cost = 16384 * (4 if phase else 1) / LINK_RATE
        return Message(("w", v, phase, j), {link: cost}, (0, phase), start, wait, then, sent)

    w_names = [(kind, v, phase, j) for kind in ("w", "wp") for v in range(4) for phase in (0, 1) for j in range(3)]

    loads_in[0].wait()
    xt4[x, y] = x_own[...].T
    loads_in[1].wait()
    pl.semaphore_wait(barrier, 30)
    for u in range(len(UNITS)):
        x_begin(u)
    for h in range(len(CHUNKS)):
        ring_begin("y", h)
    plan.poll()

    loads_in[2].wait()
    loads_in[3].wait()

    def own_left(i, carry):
        rows = pl.ds(pl.multiple_of(i * 128, 128), 128)
        parts = jnp.concatenate(split(psi[rows, :], 3), axis=0)
        both = dot(parts, xt4[x, y])
        total = both[0:128] + both[128:256] + both[256:384]
        a_part[pl.ds(pl.multiple_of(i * 8, 8), 8)] = total.reshape(8, 16, TOK)
        return carry

    lax.fori_loop(0, 2, own_left, 0)
    parts = jnp.concatenate(split(om[...], 3), axis=1)
    both = dot(yf[row], parts)
    w_part[...] = (both[:, 0:128] + both[:, 128:256] + both[:, 256:384]).reshape(16, 16, RY)
    plan.now += 4.0

    def loop_row(run):
        def body(j, carry):
            run((row + j) % 16)
            return carry

        lax.fori_loop(1, 16, body, 0)

    def loop_col(run):
        def body(j, carry):
            run((col + j) % 16)
            return carry

        lax.fori_loop(1, 16, body, 0)

    def slot_of(t):
        return 8 * (t % 2) + t // 2

    def rs_left(t):
        return remote(a_part.at[slot_of(t)], a_in.at[me_row], rs_send.at[0, slot_of(t)], rs_recv.at[0, me_row], (t, col))

    def rs_left_in(t):
        here = a_in.at[slot_of(t)]
        return remote(here, here, rs_send.at[0, slot_of(t)], rs_recv.at[0, slot_of(t)], (t, col))

    def rs_right(c):
        return remote(w_part.at[c], w_in.at[col], rs_send.at[1, c], rs_recv.at[1, col], (row, c))

    def rs_right_in(c):
        return remote(w_in.at[c], w_in.at[c], rs_send.at[1, c], rs_recv.at[1, c], (row, c))

    plan.launch(Message(
        ("rs", 1), {link: 1.4 for link in ("x+", "x-", "y+", "y-")}, (0,),
        lambda: loop_col(lambda c: rs_right(c).start()), lambda: loop_col(lambda c: rs_right_in(c).wait_recv()),
        None, lambda: loop_col(lambda c: rs_right(c).wait_send()), 3.5,
    ))
    plan.launch(Message(
        ("rs", 0), {link: 5.6 for link in ("z+", "z-")}, (0,),
        lambda: loop_row(lambda t: rs_left(t).start()), lambda: loop_row(lambda t: rs_left_in(t).wait_recv()),
        None, lambda: loop_row(lambda t: rs_left(t).wait_send()), 3.5,
    ))

    def ga(c):
        return remote(ar.at[col], ar.at[col], ga_send.at[c], ga_recv.at[col], (row, c))

    def ga_in(c):
        return remote(ar.at[c], ar.at[c], ga_send.at[c], ga_recv.at[c], (row, c))

    def gw(t):
        here = wf.at[x, y, k, z]
        return remote(here, here, gw_send.at[t], gw_recv.at[z], (2 * t + k, col))

    def gw_in(t):
        there = wf.at[x, y, k, t]
        return remote(there, there, gw_send.at[t], gw_recv.at[t], (2 * t + k, col))

    def loop_z(run):
        def body(j, carry):
            run((z + j) % 8)
            return carry

        lax.fori_loop(1, 8, body, 0)

    def gc(t):
        return remote(c_all.at[me_row], c_all.at[me_row], gc_send.at[slot_of(t)], gc_recv.at[me_row], (t, col))

    def gc_in(t):
        here = c_all.at[slot_of(t)]
        return remote(here, here, gc_send.at[slot_of(t)], gc_recv.at[slot_of(t)], (t, col))

    last = len(CHUNKS) - 1
    last_cols = pl.ds(CHUNK_AT[last], CHUNKS[last])

    def gp(t):
        here = p_all.at[k, z, :, last_cols]
        return remote(here, here, gp_send.at[slot_of(t)], gp_recv.at[me_row], (t, col))

    def gp_in(t):
        there = p_all.at[t % 2, t // 2, :, last_cols]
        return remote(there, there, gp_send.at[slot_of(t)], gp_recv.at[slot_of(t)], (t, col))

    own_half = wf.at[x, y, k]
    their_half = wf.at[x, y, 1 - k]
    half_out = remote(own_half, own_half, own_send, own_recv, (partner, col))
    half_in = remote(their_half, their_half, own_send, own_recv, (partner, col))

    def reduce_right():
        total = lax.fori_loop(1, 16, lambda j, sum_now: sum_now + w_in[(col + j) % 16], w_part[col])
        wf[x, y, k, z] = total

    def reduce_left():
        total = lax.fori_loop(1, 16, lambda j, sum_now: sum_now + a_in[slot_of((row + j) % 16)], a_part[me_row])
        ar[col] = total

    def send_right():
        plan.launch(Message(
            ("gw",), {"z+": 1.4, "z-": 1.4}, (0,),
            lambda: loop_z(lambda t: gw(t).start()), lambda: loop_z(lambda t: gw_in(t).wait_recv()),
            w_ring, lambda: loop_z(lambda t: gw(t).wait_send()), 3.5,
        ))

    def w_ring():
        for v in range(4):
            for phase in (0,):
                plan.post(w_message(v, phase, 0))
                plan.post(w_message(v, phase, 1))
        plan.post(Message(("wh",), {"p": 0.5}, (0,), half_out.start, half_in.wait_recv, None, half_out.wait_send))

    def send_left():
        plan.launch(Message(
            ("ga",), {link: 2.8 for link in ("x+", "x-", "y+", "y-")}, (0,),
            lambda: loop_col(lambda c: ga(c).start()), lambda: loop_col(lambda c: ga_in(c).wait_recv()),
            None, lambda: loop_col(lambda c: ga(c).wait_send()), 3.5,
        ))

    plan.task("reduce_right", [("rs", 1)], (0,), 0.4, lambda: (reduce_right(), send_right()))
    plan.task("reduce_left", [("rs", 0)], (0,), 0.4, lambda: (reduce_left(), send_left()))
    for v in range(4):
        plan.task(
            ("line", v), [("w", v, 0, j) for j in range(3)], (0,), 0.0,
            lambda v=v: (plan.post(w_message(v, 1, 0)), plan.post(w_message(v, 1, 1))),
        )

    def parts_left():
        for b in range(16):
            ahl[b] = jnp.concatenate(split(ar[b], 3), axis=0)

    def parts_right(quarter):
        def body(i, carry):
            b = quarter * 4 + i
            whl[b] = jnp.concatenate(split(wf[:, :, b % 2, b // 2].reshape(TOK, RY), 3), axis=1)
            return carry

        lax.fori_loop(0, 4, body, 0)

    def left_rows(parts):
        return jnp.concatenate([ahl[b, 0:16 * parts, :] for b in range(16)], axis=1)

    def core_rows():
        both = dot(left_rows(3), whl[...].reshape(16 * TOK, 3 * RY))
        total = both[0:16] + both[16:32] + both[32:48]
        c_all[me_row] = total[:, 0:RY] + total[:, RY:2 * RY] + total[:, 2 * RY:]

    def send_core():
        plan.launch(Message(
            ("gc",), {"z+": 2.8, "z-": 2.8}, (0,),
            lambda: loop_row(lambda t: gc(t).start()), lambda: loop_row(lambda t: gc_in(t).wait_recv()),
            None, lambda: loop_row(lambda t: gc(t).wait_send()), 3.5,
        ))

    plan.task("parts_left", [("ga",)], (1,), 0.3, parts_left)
    needs_w = w_names + [("wh",), ("gw",)]
    for quarter in range(4):
        plan.task(("parts", quarter), needs_w, (0, 1), 0.3, lambda quarter=quarter: parts_right(quarter))
    all_parts = ["parts_left"] + [("parts", quarter) for quarter in range(4)]
    plan.task("core_rows", all_parts, (0, 2), 1.0, lambda: (core_rows(), send_core()))

    def core_t():
        return c_all[...].reshape(RZ, RY).T

    def gram():
        inv_ref[...] = dot(core_t(), c_all[...].reshape(RZ, RY), HIGHEST)

    def pivots(begin):
        lanes = lax.broadcasted_iota(jnp.int32, (RY, RY), 1)
        subs = lax.broadcasted_iota(jnp.int32, (RY, RY), 0)

        def pivot(i, carry):
            now = inv_ref[...]
            line = inv_ref[pl.ds(i, 1), :]
            at_lane = lanes == i
            across = jnp.sum(jnp.where(at_lane, now, 0.0), axis=1, keepdims=True)
            head = jnp.sum(jnp.where(at_lane[0:1], line, 0.0), axis=1, keepdims=True)
            scaled = line / head
            inner = now - across * scaled
            on_line = jnp.where(at_lane, 1.0 / head, scaled)
            off_line = jnp.where(at_lane, -across / head, inner)
            inv_ref[...] = jnp.where(subs == i, on_line, off_line)
            return carry

        lax.fori_loop(begin, begin + 16, pivot, 0)

    def core_map():
        map_ref[...] = dot(inv_ref[...], core_t(), HIGHEST)

    plan.task("gram", [("gc",)], (0, 3), 0.7, gram)
    before = "gram"
    for begin in range(0, RY, 16):
        plan.task(("pivots", begin), [before], (0, 4), 1.1, lambda begin=begin: pivots(begin))
        before = ("pivots", begin)
    plan.task("map", [before], (0, 5), 0.6, core_map)

    def unit_rows(u):
        rows = pl.ds(UNIT_AT[u], UNITS[u])
        return jnp.concatenate([xt4[b // 4, b % 4, rows, :] for b in range(16)], axis=1)

    def right_product(u):
        both = dot(unit_rows(u), whl[:, :, 0:2 * RY].reshape(16 * TOK, 2 * RY))
        q_ref[pl.ds(UNIT_AT[u], UNITS[u]), :] = both[:, 0:RY] + both[:, RY:]

    def chunk(h):
        return yf[:, :, pl.ds(CHUNK_AT[h], CHUNKS[h])].reshape(16 * TOK, CHUNKS[h])

    def g_out(u, h):
        at = (pl.ds(UNIT_AT[u], UNITS[u]), pl.ds(CHUNK_AT[h], CHUNKS[h]))
        return pltpu.make_async_copy(g_acc.at[at], g_hbm.at[at], out_sem.at[u, h])

    def tile(u, h):
        g_acc[pl.ds(UNIT_AT[u], UNITS[u]), pl.ds(CHUNK_AT[h], CHUNKS[h])] = dot(unit_rows(u), chunk(h))

    def tile_out(u, h):
        g_out(u, h).start()
        plan.sent.append(lambda: g_out(u, h).wait())

    def left_product(h):
        both = dot(left_rows(2), chunk(h))
        p_all[k, z, :, pl.ds(CHUNK_AT[h], CHUNKS[h])] = both[0:16] + both[16:32]

    def left_out(h):
        if h < last:
            ring_begin("p", h)
        else:
            plan.launch(Message(
                ("gp",), {"z+": 2.8, "z-": 2.8}, (0,),
                lambda: loop_row(lambda t: gp(t).start()), lambda: loop_row(lambda t: gp_in(t).wait_recv()),
                None, lambda: loop_row(lambda t: gp(t).wait_send()), 3.5,
            ))

    def project(h):
        cols = pl.ds(CHUNK_AT[h], CHUNKS[h])
        r_ref[:, cols] = dot(map_ref[...], p_all[:, :, :, cols].reshape(RZ, CHUNKS[h]), HIGHEST)

    def width(n):
        return (n + 255) // 256

    for u in range(len(UNITS)):
        plan.task(("q", u), x_names(u) + all_parts, (3, u), UNITS[u] * 2.75e-3, lambda u=u: right_product(u))
        for h in range(len(CHUNKS)):
            plan.task(
                ("g", u, h), x_names(u) + ring_names("y", h), (2, max(u, h), u), UNITS[u] * width(CHUNKS[h]) * 2.75e-3,
                lambda u=u, h=h: (tile(u, h), tile_out(u, h)),
            )
    for h in range(len(CHUNKS)):
        plan.task(
            ("pr", h), ring_names("y", h) + ["parts_left"], (1, h), 0.6 * width(CHUNKS[h]),
            lambda h=h: (left_product(h), left_out(h)),
        )
        gathered = ring_names("p", h) if h < last else [("gp",)]
        plan.task(("r", h), gathered + [("pr", h), "map"], (1, 9), 0.3 * width(CHUNKS[h]), lambda h=h: project(h))

    plan.run(LOG)
    p_out = pltpu.make_async_copy(p_all, p_hbm, local_sem.at[0])
    p_out.start()
    for sent in plan.sent:
        sent()
    p_out.wait()


LOG = None


def exchange(inputs, out_grads, om, psi):
    dma = pltpu.SemaphoreType.DMA
    n_u, n_h = len(UNITS), len(CHUNKS)
    anywhere = pl.BlockSpec(memory_space=pl.ANY)
    local = pl.BlockSpec(memory_space=pltpu.VMEM)
    return pl.pallas_call(
        exchange_kernel,
        name="exchange",
        out_shape=(
            jax.ShapeDtypeStruct((BLOCK, RY), F32),
            jax.ShapeDtypeStruct((RY, BLOCK), F32),
            jax.ShapeDtypeStruct((2, 8, 16, BLOCK), F32),
            jax.ShapeDtypeStruct((BLOCK, BLOCK), F32),
        ),
        in_specs=[anywhere] * 4,
        out_specs=(local, local, anywhere, anywhere),
        scratch_shapes=[
            pltpu.VMEM((4, 4, BLOCK, TOK), BF16),
            pltpu.VMEM((16, TOK, BLOCK), BF16),
            pltpu.VMEM((4, 4, 2, 8, 16, RY), F32),
            pltpu.VMEM((16, 16, TOK), F32),
            pltpu.VMEM((16, 48, TOK), BF16),
            pltpu.VMEM((16, TOK, 3 * RY), BF16),
            pltpu.VMEM((BLOCK, BLOCK), F32),
            pltpu.VMEM((2, 8, 16, BLOCK), F32),
            pltpu.VMEM((16, 16, RY), F32),
            pltpu.VMEM((RY, RZ), F32),
            pltpu.VMEM((TOK, BLOCK), BF16),
            pltpu.VMEM((BLOCK, RY), F32),
            pltpu.VMEM((RZ, BLOCK), F32),
            pltpu.VMEM((16, 16, TOK), F32),
            pltpu.VMEM((16, 16, RY), F32),
            pltpu.VMEM((16, 16, TOK), F32),
            pltpu.VMEM((16, 16, RY), F32),
            pltpu.VMEM((RY, RY), F32),
            dma((2, 16)), dma((2, 16)),
            dma((16,)), dma((16,)),
            dma((8,)), dma((8,)),
            dma((16,)), dma((16,)),
            dma((16,)), dma((16,)),
            dma((n_u, 2, 15)), dma((n_u, 2, 15)),
            dma((4, 2, 3)), dma((4, 2, 3)),
            dma((4, 2, 3)), dma((4, 2, 3)),
            dma((n_h, 2, 4)), dma((n_h, 2, 4)),
            dma((n_h, 2, 5)), dma((n_h, 2, 5)),
            dma((n_h, 2, 4)), dma((n_h, 2, 4)),
            dma((n_h, 2, 5)), dma((n_h, 2, 5)),
            dma, dma, dma((4,)), dma((n_u, n_h)),
        ],
        compiler_params=pltpu.CompilerParams(
            collective_id=0, has_side_effects=True, vmem_limit_bytes=62 * 1024 * 1024
        ),
    )(inputs, out_grads, om, psi)


def finish_kernel(g_ref, q_ref, r_ref, p_ref, res_ref, qo_ref, po_ref):
    q_high, q_low = split(q_ref[...], 2)
    r_high, r_low = split(r_ref[...], 2)
    left = jnp.concatenate([q_high, q_low, q_high], axis=1)
    right = jnp.concatenate([r_high, r_high, r_low], axis=0)
    res_ref[...] = g_ref[...] - dot(left, right)
    po_ref[...] = p_ref[...]

    @pl.when(pl.program_id(0) == 0)
    def _():
        qo_ref[...] = q_ref[...]


def finish(g, q, r, p):
    def cols(height):
        return pl.BlockSpec((height, FINISH_COLS), lambda i: (0, i))

    whole = pl.BlockSpec((BLOCK, RY), lambda i: (0, 0))
    return pl.pallas_call(
        finish_kernel,
        name="finish",
        grid=(BLOCK // FINISH_COLS,),
        out_shape=(
            jax.ShapeDtypeStruct((BLOCK, BLOCK), F32),
            jax.ShapeDtypeStruct((BLOCK, RY), F32),
            jax.ShapeDtypeStruct((RZ, BLOCK), F32),
        ),
        in_specs=[cols(BLOCK), whole, cols(RY), cols(RZ)],
        out_specs=(cols(BLOCK), whole, cols(RZ)),
    )(g, q, r, p)


def per_device(inputs, out_grads, range_test, corange_test):
    q, r, p, g = exchange(inputs, out_grads, range_test, corange_test)
    residual, q, p = finish(g, q, r, p.reshape(RZ, BLOCK))
    return (q, p, residual)


def solution(mesh):
    placed = (P("col", "row"), P("row", "col"), P("col", None), P(None, "row"))
    return jax.shard_map(
        per_device,
        mesh=mesh,
        in_specs=placed,
        out_specs=(P("row", None), P(None, "col"), P("row", "col")),
        check_vma=False,
    )
```

time: 438 us -> 121 us (0.28)
  waiting for transfers between devices: 345 us -> 0 us
  Pallas kernels: 0 us -> 120 us
  matrix products: 50.3 us -> 0 us
  other arithmetic: 23.1 us -> 0 us
  between operations: 13.9 us -> 0.67 us
  local copies, waits for them, and re-layouts: 5.95 us -> 0 us
    psum x2 -> x0, waiting for transfers between devices: 194 us -> none  [the longest x1 115 us: per_device(): corange_sketch = lax.psum(exact_product(corange_test, gradient), 'row')]
    all_gather x2 -> x0, waiting for transfers between devices: 149 us -> none  [the longest x1 86 us: per_device(): lax.all_gather(inputs, 'col', axis=0, tiled=True)]
    pallas_call x0 -> x2, Pallas kernels: none -> 120 us  [the longest x1 112 us: exchange(): pl.pallas_call(exchange_kernel, name='exchange', out_shape=(jax.ShapeDtyp...]
    dot_general x7 -> x0, matrix products: 48.8 us -> none  [the longest x5 30.5 us: exact_product(): jnp.dot(left_side, right_side, precision=highest, preferred_element_type=...]
    another operation x5 -> x0, other arithmetic: 23.1 us -> none  [the longest x3 12.6 us: per_device(): factor_low = jnp.linalg.cholesky(gram_matrix)]
    unnamed x10 -> x0, local copies, waits for them, and re-layouts: 5.86 us -> none
  transfers between devices with their start and end apart: 4 -> 0, of which waited for: 4 -> 0; matrix products, arithmetic and copies ran while one was open for 3% -> 0% of each run, Pallas kernels for 0% -> 0%
where the time goes in v2:
time: 121 us; the launch traced here: 120 us
  Pallas kernels  120 us (99%)
    pallas_call x1, Pallas kernels, exchange(): pl.pallas_call(exchange_kernel, name='exchange', out_shape=(jax.ShapeDtyp...  112 us
    pallas_call x1, Pallas kernels, finish(): pl.pallas_call(finish_kernel, name='finish', grid=(BLOCK // FINISH_COLS,)...  8.13 us

profile of v2, /device:TPU:1, one launch (start us, length us, event | category | flops | bytes accessed | tf_op | source)
XLA Modules:
  0.0 120.4 jit_solution(4454885700141471621)
XLA Ops:
  0.6 111.6 %exchange.1 = (f32[1152,128]{1,0:T(8,128)}, f32[128,1152]{1,0:T(8,128)}, f32[2,8,16,1152]{3,2,1,0:T(8,128)}, f32[1152,1152]{1,0:T(8,128)}) custom-call(bf16[256,1152]{1,0:T(8,128)(2,1)} %x_hbm.1, bf16[256,1152]{1,0:T(8,128)(2,1)} %y_hbm.1, f32[1152,128]{1,0:T(8,128)} %om_hbm.1, f32[256,1152]{1,0:T(8,128)} %psi_hbm.1), custom_call_target="tpu_custom_call" | custom-call | tf_op jit(solution)/shard_map/exchange/pallas_call | solution.py:633
  112.3 8.1 %finish.1 = (f32[1152,1152]{1,0:T(8,128)}, f32[1152,128]{1,0:T(8,128)}, f32[256,1152]{1,0:T(8,128)}) custom-call(f32[1152,1152]{1,0:T(8,128)} %get-tuple-element.10.g_ref, f32[1152,128]{1,0:T(8,128)} %get-tuple-element.11.q_ref, f32[128,1152]{1,0:T(8,128)} %get-tuple-element.12.r_ref, f32[256,1152]{1,0:T(8,128)} %bitcast.1), custom_call_target="tpu_custom_call" | custom-call | tf_op jit(solution)/shard_map/finish/pallas_call | solution.py:701

commit v3 on v2

--- a/solution.py
+++ b/solution.py
@@ -19,6 +19,7 @@
 UNITS = (384, 384, 256, 128)
 CHUNKS = (512, 512, 128)
 FINISH_COLS = 384
+EXCHANGE_LIMIT, FINISH_LIMIT = 42, 18
 
 LINK_RATE = 46500.0
 PARTNER_RATE = 150000.0
@@ -531,20 +532,37 @@
         lanes = lax.broadcasted_iota(jnp.int32, (RY, RY), 1)
         subs = lax.broadcasted_iota(jnp.int32, (RY, RY), 0)
 
-        def pivot(i, carry):
+        def pivot(step, carry):
+            i = 2 * step
             now = inv_ref[...]
-            line = inv_ref[pl.ds(i, 1), :]
-            at_lane = lanes == i
-            across = jnp.sum(jnp.where(at_lane, now, 0.0), axis=1, keepdims=True)
-            head = jnp.sum(jnp.where(at_lane[0:1], line, 0.0), axis=1, keepdims=True)
-            scaled = line / head
-            inner = now - across * scaled
-            on_line = jnp.where(at_lane, 1.0 / head, scaled)
-            off_line = jnp.where(at_lane, -across / head, inner)
-            inv_ref[...] = jnp.where(subs == i, on_line, off_line)
+            line_a = inv_ref[pl.ds(i, 1), :]
+            line_b = inv_ref[pl.ds(i + 1, 1), :]
+            at_a, at_b = lanes == i, lanes == i + 1
+            on_a, on_b = subs == i, subs == i + 1
+
+            def pick(mask, value):
+                return jnp.sum(jnp.where(mask, value, 0.0), axis=1, keepdims=True)
+
+            over_a, over_b = pick(at_a, now), pick(at_b, now)
+            aa, ab = pick(at_a[0:1], line_a), pick(at_b[0:1], line_a)
+            ba, bb = pick(at_a[0:1], line_b), pick(at_b[0:1], line_b)
+            head = 1.0 / aa
+            ratio_a, ratio_b = ba * head, ab * head
+            rest = 1.0 / (bb - ba * ratio_b)
+            low, high = -ratio_a * rest, -ratio_b * rest
+            top = head + ratio_b * rest * ratio_a
+            row_a = top * line_a + high * line_b
+            row_b = low * line_a + rest * line_b
+            col_a = over_a * top + over_b * low
+            col_b = over_a * high + over_b * rest
+            inner = now - over_a * row_a - over_b * row_b
+            inner = jnp.where(at_a, -col_a, jnp.where(at_b, -col_b, inner))
+            row_a = jnp.where(at_a[0:1], top, jnp.where(at_b[0:1], high, row_a))
+            row_b = jnp.where(at_a[0:1], low, jnp.where(at_b[0:1], rest, row_b))
+            inv_ref[...] = jnp.where(on_a, row_a, jnp.where(on_b, row_b, inner))
             return carry
 
-        lax.fori_loop(begin, begin + 16, pivot, 0)
+        lax.fori_loop(begin // 2, begin // 2 + 8, pivot, 0)
 
     def core_map():
         map_ref[...] = dot(inv_ref[...], core_t(), HIGHEST)
@@ -552,7 +570,7 @@
     plan.task("gram", [("gc",)], (0, 3), 0.7, gram)
     before = "gram"
     for begin in range(0, RY, 16):
-        plan.task(("pivots", begin), [before], (0, 4), 1.1, lambda begin=begin: pivots(begin))
+        plan.task(("pivots", begin), [before], (0, 4), 0.7, lambda begin=begin: pivots(begin))
         before = ("pivots", begin)
     plan.task("map", [before], (0, 5), 0.6, core_map)
 
@@ -574,13 +592,15 @@
     def tile(u, h):
         g_acc[pl.ds(UNIT_AT[u], UNITS[u]), pl.ds(CHUNK_AT[h], CHUNKS[h])] = dot(unit_rows(u), chunk(h))
 
+    def first_tile(h):
+        cols = pl.ds(CHUNK_AT[h], CHUNKS[h])
+        both = dot(jnp.concatenate([unit_rows(0), left_rows(2)], axis=0), chunk(h))
+        g_acc[pl.ds(0, UNITS[0]), cols] = both[0:UNITS[0]]
+        p_all[k, z, :, cols] = both[UNITS[0]:UNITS[0] + 16] + both[UNITS[0] + 16:]
+
     def tile_out(u, h):
         g_out(u, h).start()
         plan.sent.append(lambda: g_out(u, h).wait())
-
-    def left_product(h):
-        both = dot(left_rows(2), chunk(h))
-        p_all[k, z, :, pl.ds(CHUNK_AT[h], CHUNKS[h])] = both[0:16] + both[16:32]
 
     def left_out(h):
         if h < last:
@@ -601,15 +621,16 @@
 
     for u in range(len(UNITS)):
         plan.task(("q", u), x_names(u) + all_parts, (3, u), UNITS[u] * 2.75e-3, lambda u=u: right_product(u))
-        for h in range(len(CHUNKS)):
+        for h in range(len(CHUNKS)) if u else ():
             plan.task(
                 ("g", u, h), x_names(u) + ring_names("y", h), (2, max(u, h), u), UNITS[u] * width(CHUNKS[h]) * 2.75e-3,
                 lambda u=u, h=h: (tile(u, h), tile_out(u, h)),
             )
     for h in range(len(CHUNKS)):
         plan.task(
-            ("pr", h), ring_names("y", h) + ["parts_left"], (1, h), 0.6 * width(CHUNKS[h]),
-            lambda h=h: (left_product(h), left_out(h)),
+            ("pr", h), x_names(0) + ring_names("y", h) + ["parts_left"], (1, h),
+            (UNITS[0] + 32) * width(CHUNKS[h]) * 2.75e-3,
+            lambda h=h: (first_tile(h), left_out(h), tile_out(0, h)),
         )
         gathered = ring_names("p", h) if h < last else [("gp",)]
         plan.task(("r", h), gathered + [("pr", h), "map"], (1, 9), 0.3 * width(CHUNKS[h]), lambda h=h: project(h))
@@ -639,7 +660,7 @@
             jax.ShapeDtypeStruct((2, 8, 16, BLOCK), F32),
             jax.ShapeDtypeStruct((BLOCK, BLOCK), F32),
         ),
-        in_specs=[anywhere] * 4,
+        in_specs=[pl.BlockSpec(memory_space=pltpu.HBM)] * 4,
         out_specs=(local, local, anywhere, anywhere),
         scratch_shapes=[
             pltpu.VMEM((4, 4, BLOCK, TOK), BF16),
@@ -675,7 +696,7 @@
             dma, dma, dma((4,)), dma((n_u, n_h)),
         ],
         compiler_params=pltpu.CompilerParams(
-            collective_id=0, has_side_effects=True, vmem_limit_bytes=62 * 1024 * 1024
+            collective_id=0, has_side_effects=True, vmem_limit_bytes=EXCHANGE_LIMIT * 1024 * 1024
         ),
     )(inputs, out_grads, om, psi)
 
@@ -709,6 +730,7 @@
         ),
         in_specs=[cols(BLOCK), whole, cols(RY), cols(RZ)],
         out_specs=(cols(BLOCK), whole, cols(RZ)),
+        compiler_params=pltpu.CompilerParams(vmem_limit_bytes=FINISH_LIMIT * 1024 * 1024),
     )(g, q, r, p)
 
 

time: 121 us -> 118 us (0.975)
  Pallas kernels: 120 us -> 113 us
  local copies, waits for them, and re-layouts: 0 us -> 4.45 us
    unnamed x0 -> x8, local copies, waits for them, and re-layouts: none -> 4.45 us
    pallas_call x1, Pallas kernels: 8.13 us -> 4.57 us  [finish(): pl.pallas_call(finish_kernel, name='finish', grid=(BLOCK // FINISH_COLS,)...]
    pallas_call x1, Pallas kernels: 112 us -> 108 us  [exchange(): pl.pallas_call(exchange_kernel, name='exchange', out_shape=(jax.ShapeDtyp...]
where the time goes in v3:
time: 118 us
  Pallas kernels  113 us (96%)
  local copies, waits for them, and re-layouts  4.45 us (4%)
    pallas_call x1, Pallas kernels, exchange(): pl.pallas_call(exchange_kernel, name='exchange', out_shape=(jax.ShapeDtyp...  108 us
    pallas_call x1, Pallas kernels, finish(): pl.pallas_call(finish_kernel, name='finish', grid=(BLOCK // FINISH_COLS,)...  4.57 us
    unnamed x8, local copies, waits for them, and re-layouts  4.45 us

profile of v3, /device:TPU:1, one launch (start us, length us, event | category | flops | bytes accessed | tf_op | source)
XLA Modules:
  0.0 118.0 jit_solution(3232769808030013180)
XLA Ops:
  0.6 0.0 copy-start
  0.6 1.3 %copy-done = f32[256,1152]{1,0:T(8,128)S(1)} copy-done((f32[256,1152]{1,0:T(8,128)S(1)}, f32[256,1152]{1,0:T(8,128)}, u32[]{:S(2)}) %copy-start) | copy-done | bytes 1179672
  1.9 0.0 copy-start.1
  1.9 1.1 copy-done.1
  3.0 0.0 copy-start.2
  3.0 1.1 copy-done.2
  4.0 0.0 copy-start.3
  4.0 1.1 copy-done.3
  5.1 108.3 %exchange.1 = (f32[1152,128]{1,0:T(8,128)S(1)}, f32[128,1152]{1,0:T(8,128)S(1)}, f32[2,8,16,1152]{3,2,1,0:T(8,128)S(1)}, f32[1152,1152]{1,0:T(8,128)S(1)}) custom-call(bf16[256,1152]{1,0:T(8,128)(2,1)S(1)} %copy-done.1, bf16[256,1152]{1,0:T(8,128)(2,1)S(1)} %copy-done.2, f32[1152,128]{1,0:T(8,128)S(1)} %copy-done.3, f32[256,1152]{1,0:T(8,128)S(1)} %copy-done), custom_call_target="tpu_custom_call" | custom-call | tf_op jit(solution)/shard_map/exchange/pallas_call | solution.py:654
  113.4 4.6 %finish.1 = (f32[1152,1152]{1,0:T(8,128)}, f32[1152,128]{1,0:T(8,128)}, f32[256,1152]{1,0:T(8,128)}) custom-call(f32[1152,1152]{1,0:T(8,128)S(1)} %get-tuple-element.10.g_ref, f32[1152,128]{1,0:T(8,128)S(1)} %get-tuple-element.11.q_ref, f32[128,1152]{1,0:T(8,128)S(1)} %get-tuple-element.12.r_ref, f32[256,1152]{1,0:T(8,128)S(1)} %bitcast.1), custom_call_target="tpu_custom_call" | custom-call | tf_op jit(solution)/shard_map/finish/pallas_call | solution.py:722
Async XLA Ops:
  0.6 1.3 %copy-start = (f32[256,1152]{1,0:T(8,128)S(1)}, f32[256,1152]{1,0:T(8,128)}, u32[]{:S(2)}) copy-start(f32[256,1152]{1,0:T(8,128)} %psi_hbm.1) | copy-start | bytes 3538948
  1.9 1.1 copy-start.1
  3.0 1.1 copy-start.2
  4.0 1.1 copy-start.3

commit v4 on v3

--- a/solution.py
+++ b/solution.py
@@ -120,7 +120,7 @@
     x_hbm, y_hbm, om_hbm, psi_hbm,
     q_ref, r_ref, p_hbm, g_hbm,
     xt4, yf, wf, ar, ahl, whl, g_acc, p_all, c_all, map_ref,
-    x_own, om, psi, a_part, w_part, a_in, w_in, inv_ref,
+    x_own, om, psi, a_part, w_part, a_pre, a_in, w_in, inv_ref,
     rs_send, rs_recv, ga_send, ga_recv, gw_send, gw_recv, gc_send, gc_recv, gp_send, gp_recv,
     x_send, x_recv, w_send, w_recv, wp_send, wp_recv,
     z_send, z_recv, yp_send, yp_recv, p_send, p_recv, pp_send, pp_recv,
@@ -383,12 +383,23 @@
     def slot_of(t):
         return 8 * (t % 2) + t // 2
 
+    mine = pl.ds(pl.multiple_of(8 * k, 8), 8)
+    theirs = pl.ds(pl.multiple_of(8 * (1 - k), 8), 8)
+
+    def loop_z(run):
+        def body(j, carry):
+            run((z + j) % 8)
+            return carry
+
+        lax.fori_loop(1, 8, body, 0)
+
+    pre_out = remote(a_part.at[theirs], a_pre, rs_send.at[0, 8], rs_recv.at[0, 8], (partner, col))
+
     def rs_left(t):
-        return remote(a_part.at[slot_of(t)], a_in.at[me_row], rs_send.at[0, slot_of(t)], rs_recv.at[0, me_row], (t, col))
+        return remote(a_part.at[8 * k + t], a_in.at[z], rs_send.at[0, t], rs_recv.at[0, z], (2 * t + k, col))
 
     def rs_left_in(t):
-        here = a_in.at[slot_of(t)]
-        return remote(here, here, rs_send.at[0, slot_of(t)], rs_recv.at[0, slot_of(t)], (t, col))
+        return remote(a_in.at[t], a_in.at[t], rs_send.at[0, t], rs_recv.at[0, t], (2 * t + k, col))
 
     def rs_right(c):
         return remote(w_part.at[c], w_in.at[col], rs_send.at[1, c], rs_recv.at[1, col], (row, c))
@@ -402,10 +413,18 @@
         None, lambda: loop_col(lambda c: rs_right(c).wait_send()), 3.5,
     ))
     plan.launch(Message(
-        ("rs", 0), {link: 5.6 for link in ("z+", "z-")}, (0,),
-        lambda: loop_row(lambda t: rs_left(t).start()), lambda: loop_row(lambda t: rs_left_in(t).wait_recv()),
-        None, lambda: loop_row(lambda t: rs_left(t).wait_send()), 3.5,
+        ("pre",), {"p": 0.9}, (0,), pre_out.start, pre_out.wait_recv, None, pre_out.wait_send
     ))
+
+    def scatter_left():
+        a_part[mine] = a_part[mine] + a_pre[...]
+        plan.launch(Message(
+            ("rs", 0), {link: 2.8 for link in ("z+", "z-")}, (0,),
+            lambda: loop_z(lambda t: rs_left(t).start()), lambda: loop_z(lambda t: rs_left_in(t).wait_recv()),
+            None, lambda: loop_z(lambda t: rs_left(t).wait_send()), 3.5,
+        ))
+
+    plan.task("scatter_left", [("pre",)], (0,), 0.3, scatter_left)
 
     def ga(c):
         return remote(ar.at[col], ar.at[col], ga_send.at[c], ga_recv.at[col], (row, c))
@@ -421,30 +440,26 @@
         there = wf.at[x, y, k, t]
         return remote(there, there, gw_send.at[t], gw_recv.at[t], (2 * t + k, col))
 
-    def loop_z(run):
-        def body(j, carry):
-            run((z + j) % 8)
-            return carry
-
-        lax.fori_loop(1, 8, body, 0)
-
-    def gc(t):
-        return remote(c_all.at[me_row], c_all.at[me_row], gc_send.at[slot_of(t)], gc_recv.at[me_row], (t, col))
-
-    def gc_in(t):
-        here = c_all.at[slot_of(t)]
-        return remote(here, here, gc_send.at[slot_of(t)], gc_recv.at[slot_of(t)], (t, col))
+    def spread(name, cost, piece, whole, send_sem, recv_sem):
+        def out(t):
+            return remote(piece(z), piece(z), send_sem.at[t], recv_sem.at[z], (2 * t + k, col))
+
+        def into(t):
+            return remote(piece(t), piece(t), send_sem.at[t], recv_sem.at[t], (2 * t + k, col))
+
+        half = remote(whole(k), whole(k), send_sem.at[8], recv_sem.at[8], (partner, col))
+        other = remote(whole(1 - k), whole(1 - k), send_sem.at[8], recv_sem.at[8], (partner, col))
+        plan.launch(Message(
+            (name,), {"z+": cost, "z-": cost}, (0,),
+            lambda: loop_z(lambda t: out(t).start()), lambda: loop_z(lambda t: into(t).wait_recv()),
+            lambda: plan.post(Message(
+                (name, 1), {"p": 0.4}, (0,), half.start, other.wait_recv, None, half.wait_send
+            )),
+            lambda: loop_z(lambda t: out(t).wait_send()), 3.5,
+        ))
 
     last = len(CHUNKS) - 1
     last_cols = pl.ds(CHUNK_AT[last], CHUNKS[last])
-
-    def gp(t):
-        here = p_all.at[k, z, :, last_cols]
-        return remote(here, here, gp_send.at[slot_of(t)], gp_recv.at[me_row], (t, col))
-
-    def gp_in(t):
-        there = p_all.at[t % 2, t // 2, :, last_cols]
-        return remote(there, there, gp_send.at[slot_of(t)], gp_recv.at[slot_of(t)], (t, col))
 
     own_half = wf.at[x, y, k]
     their_half = wf.at[x, y, 1 - k]
@@ -456,7 +471,7 @@
         wf[x, y, k, z] = total
 
     def reduce_left():
-        total = lax.fori_loop(1, 16, lambda j, sum_now: sum_now + a_in[slot_of((row + j) % 16)], a_part[me_row])
+        total = lax.fori_loop(1, 8, lambda j, sum_now: sum_now + a_in[(z + j) % 8], a_part[me_row])
         ar[col] = total
 
     def send_right():
@@ -509,11 +524,10 @@
         c_all[me_row] = total[:, 0:RY] + total[:, RY:2 * RY] + total[:, 2 * RY:]
 
     def send_core():
-        plan.launch(Message(
-            ("gc",), {"z+": 2.8, "z-": 2.8}, (0,),
-            lambda: loop_row(lambda t: gc(t).start()), lambda: loop_row(lambda t: gc_in(t).wait_recv()),
-            None, lambda: loop_row(lambda t: gc(t).wait_send()), 3.5,
-        ))
+        spread(
+            "gc", 1.4, lambda t: c_all.at[8 * k + t],
+            lambda kk: c_all.at[pl.ds(pl.multiple_of(8 * kk, 8), 8)], gc_send, gc_recv,
+        )
 
     plan.task("parts_left", [("ga",)], (1,), 0.3, parts_left)
     needs_w = w_names + [("wh",), ("gw",)]
@@ -567,7 +581,7 @@
     def core_map():
         map_ref[...] = dot(inv_ref[...], core_t(), HIGHEST)
 
-    plan.task("gram", [("gc",)], (0, 3), 0.7, gram)
+    plan.task("gram", [("gc",), ("gc", 1)], (0, 3), 0.7, gram)
     before = "gram"
     for begin in range(0, RY, 16):
         plan.task(("pivots", begin), [before], (0, 4), 0.7, lambda begin=begin: pivots(begin))
@@ -606,11 +620,10 @@
         if h < last:
             ring_begin("p", h)
         else:
-            plan.launch(Message(
-                ("gp",), {"z+": 2.8, "z-": 2.8}, (0,),
-                lambda: loop_row(lambda t: gp(t).start()), lambda: loop_row(lambda t: gp_in(t).wait_recv()),
-                None, lambda: loop_row(lambda t: gp(t).wait_send()), 3.5,
-            ))
+            spread(
+                "gp", 1.4, lambda t: p_all.at[k, t, :, last_cols],
+                lambda kk: p_all.at[kk, :, :, last_cols], gp_send, gp_recv,
+            )
 
     def project(h):
         cols = pl.ds(CHUNK_AT[h], CHUNKS[h])
@@ -632,7 +645,7 @@
             (UNITS[0] + 32) * width(CHUNKS[h]) * 2.75e-3,
             lambda h=h: (first_tile(h), left_out(h), tile_out(0, h)),
         )
-        gathered = ring_names("p", h) if h < last else [("gp",)]
+        gathered = ring_names("p", h) if h < last else [("gp",), ("gp", 1)]
         plan.task(("r", h), gathered + [("pr", h), "map"], (1, 9), 0.3 * width(CHUNKS[h]), lambda h=h: project(h))
 
     plan.run(LOG)
@@ -678,7 +691,8 @@
             pltpu.VMEM((RZ, BLOCK), F32),
             pltpu.VMEM((16, 16, TOK), F32),
             pltpu.VMEM((16, 16, RY), F32),
-            pltpu.VMEM((16, 16, TOK), F32),
+            pltpu.VMEM((8, 16, TOK), F32),
+            pltpu.VMEM((8, 16, TOK), F32),
             pltpu.VMEM((16, 16, RY), F32),
             pltpu.VMEM((RY, RY), F32),
             dma((2, 16)), dma((2, 16)),

time: 118 us -> 118 us (level)
  no operation moved by 1% of the time
where the time goes in v4:
time: 118 us
  Pallas kernels  113 us (96%)
  local copies, waits for them, and re-layouts  4.45 us (4%)
    pallas_call x1, Pallas kernels, exchange(): pl.pallas_call(exchange_kernel, name='exchange', out_shape=(jax.ShapeDtyp...  108 us
    pallas_call x1, Pallas kernels, finish(): pl.pallas_call(finish_kernel, name='finish', grid=(BLOCK // FINISH_COLS,)...  4.57 us
    unnamed x8, local copies, waits for them, and re-layouts  4.45 us

profile of v4, /device:TPU:1, one launch (start us, length us, event | category | flops | bytes accessed | tf_op | source)
XLA Modules:
  0.0 118.1 jit_solution(6451084726383778923)
XLA Ops:
  0.6 0.0 copy-start
  0.6 1.3 %copy-done = f32[256,1152]{1,0:T(8,128)S(1)} copy-done((f32[256,1152]{1,0:T(8,128)S(1)}, f32[256,1152]{1,0:T(8,128)}, u32[]{:S(2)}) %copy-start) | copy-done | bytes 1179672
  1.9 0.0 copy-start.1
  1.9 1.1 copy-done.1
  3.0 0.0 copy-start.2
  3.0 1.1 copy-done.2
  4.0 0.0 copy-start.3
  4.0 1.1 copy-done.3
  5.1 108.5 %exchange.1 = (f32[1152,128]{1,0:T(8,128)S(1)}, f32[128,1152]{1,0:T(8,128)S(1)}, f32[2,8,16,1152]{3,2,1,0:T(8,128)S(1)}, f32[1152,1152]{1,0:T(8,128)S(1)}) custom-call(bf16[256,1152]{1,0:T(8,128)(2,1)S(1)} %copy-done.1, bf16[256,1152]{1,0:T(8,128)(2,1)S(1)} %copy-done.2, f32[1152,128]{1,0:T(8,128)S(1)} %copy-done.3, f32[256,1152]{1,0:T(8,128)S(1)} %copy-done), custom_call_target="tpu_custom_call" | custom-call | tf_op jit(solution)/shard_map/exchange/pallas_call | solution.py:667
  113.6 4.6 %finish.1 = (f32[1152,1152]{1,0:T(8,128)}, f32[1152,128]{1,0:T(8,128)}, f32[256,1152]{1,0:T(8,128)}) custom-call(f32[1152,1152]{1,0:T(8,128)S(1)} %get-tuple-element.10.g_ref, f32[1152,128]{1,0:T(8,128)S(1)} %get-tuple-element.11.q_ref, f32[128,1152]{1,0:T(8,128)S(1)} %get-tuple-element.12.r_ref, f32[256,1152]{1,0:T(8,128)S(1)} %bitcast.1), custom_call_target="tpu_custom_call" | custom-call | tf_op jit(solution)/shard_map/finish/pallas_call | solution.py:736
Async XLA Ops:
  0.6 1.3 %copy-start = (f32[256,1152]{1,0:T(8,128)S(1)}, f32[256,1152]{1,0:T(8,128)}, u32[]{:S(2)}) copy-start(f32[256,1152]{1,0:T(8,128)} %psi_hbm.1) | copy-start | bytes 3538948
  1.9 1.1 copy-start.1
  3.0 1.1 copy-start.2
  4.0 1.1 copy-start.3

commit v5 on v4

--- a/solution.py
+++ b/solution.py
@@ -16,7 +16,7 @@
 TOK = 256
 RY = 128
 RZ = 256
-UNITS = (384, 384, 256, 128)
+UNITS = (576, 576)
 CHUNKS = (512, 512, 128)
 FINISH_COLS = 384
 EXCHANGE_LIMIT, FINISH_LIMIT = 42, 18

time: 118 us -> 114 us (0.966); the launches traced: 118 us -> 113 us
  Pallas kernels: 113 us -> 108 us
    pallas_call x1, Pallas kernels: 108 us -> 103 us  [exchange(): pl.pallas_call(exchange_kernel, name='exchange', out_shape=(jax.ShapeDtyp...]
where the time goes in v5:
time: 114 us; the launch traced here: 113 us
  Pallas kernels  108 us (95%)
  local copies, waits for them, and re-layouts  4.45 us (4%)
    pallas_call x1, Pallas kernels, exchange(): pl.pallas_call(exchange_kernel, name='exchange', out_shape=(jax.ShapeDtyp...  103 us
    pallas_call x1, Pallas kernels, finish(): pl.pallas_call(finish_kernel, name='finish', grid=(BLOCK // FINISH_COLS,)...  4.57 us
    unnamed x8, local copies, waits for them, and re-layouts  4.45 us

profile of v5, /device:TPU:1, one launch (start us, length us, event | category | flops | bytes accessed | tf_op | source)
XLA Modules:
  0.0 112.8 jit_solution(11041857229834960480)
XLA Ops:
  0.6 0.0 copy-start
  0.6 1.3 %copy-done = f32[256,1152]{1,0:T(8,128)S(1)} copy-done((f32[256,1152]{1,0:T(8,128)S(1)}, f32[256,1152]{1,0:T(8,128)}, u32[]{:S(2)}) %copy-start) | copy-done | bytes 1179672
  1.9 0.0 copy-start.1
  1.9 1.1 copy-done.1
  3.0 0.0 copy-start.2
  3.0 1.1 copy-done.2
  4.0 0.0 copy-start.3
  4.0 1.1 copy-done.3
  5.1 103.1 %exchange.1 = (f32[1152,128]{1,0:T(8,128)S(1)}, f32[128,1152]{1,0:T(8,128)S(1)}, f32[2,8,16,1152]{3,2,1,0:T(8,128)S(1)}, f32[1152,1152]{1,0:T(8,128)S(1)}) custom-call(bf16[256,1152]{1,0:T(8,128)(2,1)S(1)} %copy-done.1, bf16[256,1152]{1,0:T(8,128)(2,1)S(1)} %copy-done.2, f32[1152,128]{1,0:T(8,128)S(1)} %copy-done.3, f32[256,1152]{1,0:T(8,128)S(1)} %copy-done), custom_call_target="tpu_custom_call" | custom-call | tf_op jit(solution)/shard_map/exchange/pallas_call | solution.py:667
  108.2 4.6 %finish.1 = (f32[1152,1152]{1,0:T(8,128)}, f32[1152,128]{1,0:T(8,128)}, f32[256,1152]{1,0:T(8,128)}) custom-call(f32[1152,1152]{1,0:T(8,128)S(1)} %get-tuple-element.10.g_ref, f32[1152,128]{1,0:T(8,128)S(1)} %get-tuple-element.11.q_ref, f32[128,1152]{1,0:T(8,128)S(1)} %get-tuple-element.12.r_ref, f32[256,1152]{1,0:T(8,128)S(1)} %bitcast.1), custom_call_target="tpu_custom_call" | custom-call | tf_op jit(solution)/shard_map/finish/pallas_call | solution.py:736
Async XLA Ops:
  0.6 1.3 %copy-start = (f32[256,1152]{1,0:T(8,128)S(1)}, f32[256,1152]{1,0:T(8,128)}, u32[]{:S(2)}) copy-start(f32[256,1152]{1,0:T(8,128)} %psi_hbm.1) | copy-start | bytes 3538948
  1.9 1.1 copy-start.1
  3.0 1.1 copy-start.2
  4.0 1.1 copy-start.3
